TPU v7x, 32 devices: a whole 2x2x4 slice. The times are simulated.
32 devices in a mesh: groups: 2 (over y), seq: 4 (over z), rep: 2 (over x), sub: 2 (over core).
Axes of the slice: x: 2, y: 2, z: 4, core: 2. Of those that a mesh axis runs over, the one named last changes fastest.
Arguments:
- queries: bfloat16 [4, 512, 32, 384], P(('groups', 'rep'), 'seq', None, 'sub'), parts along dimension 0, may hold values from -64 to 64
- grad_out: bfloat16 [4, 512, 32, 256], P(('groups', 'rep'), 'seq', None, 'sub'), parts along dimension 0, may hold values from -6 to 6
- latent_kv: bfloat16 [4, 512, 576], P(('groups', 'rep'), 'seq'), parts along dimension 0, may hold values from -24 to 24
- key_up: bfloat16 [32, 2, 128, 512], P('seq', 'sub'), may hold values from -0.25 to 0.25
- value_up: bfloat16 [32, 2, 512, 128], P('seq', 'sub'), may hold values from -0.25 to 0.25
- key_blocks: int32 [4, 4, 3], P(('groups', 'rep')), parts along dimension 0, may hold values from 0 to 3, as said below
- block_counts: int32 [4, 4], P(('groups', 'rep')), parts along dimension 0, may hold values from 1 to 3, as said below
Outputs:
- grad_queries: bfloat16 [4, 512, 32, 384], P(('groups', 'rep'), 'seq', None, 'sub'), parts along dimension 0
- grad_latent: float32 [4, 512, 576], P(('groups', 'rep'), 'seq', 'sub'), parts along dimension 0
- grad_key_up: float32 [64, 2, 128, 512], P(('groups', 'seq'), 'sub', 'rep'), parts along dimension 0
- grad_value_up: float32 [64, 2, 512, 128], P(('groups', 'seq'), 'sub', 'rep'), parts along dimension 0
There are 2 independent parts, one for each index of `groups`. A program takes and returns all parts, laid end to end along the dimension named above; an argument that names none is the same for every part. Nothing has to cross between parts.
Inputs may be any that keep to these rules, and one draw needn't show every extreme that they name: `key_blocks`: row b of a sequence lists key blocks for query block b: its first entry is b, its first block_counts[b] entries are distinct and none exceeds b, and the remaining entries equal b. `block_counts`: query block b lists at most min(b + 1, 3) key blocks; the last query block of each sequence lists exactly 3.
All inputs are finite; a program needn't handle non-finite values.
Results may differ from a plain program's by a relative error of at most 0.012.
Values may be sent and summed in bfloat16 or wider, within the bound.
A program may use at most 128 MiB of HBM per device.

v0:
```python
import math

import jax
import jax.numpy as jnp
from jax import lax
from jax.sharding import PartitionSpec as P

BLK = 128


def head_backward(
    head_queries, head_grads, latent, key_weight, value_weight, slot_list, count_list, block_rows
):
    length = head_queries.shape[0]
    latent_width = key_weight.shape[1]
    nope_width = key_weight.shape[0]
    query_width = head_queries.shape[1]
    value_width = head_grads.shape[1]
    block_count = length // block_rows
    slot_count = slot_list.shape[1]
    factor = 1.0 / math.sqrt(query_width)
    compressed = latent[:, :latent_width]
    key_nope = jnp.einsum(
        "tl,dl->td", compressed, key_weight, preferred_element_type=jnp.float32
    ).astype(jnp.bfloat16)
    values = jnp.dot(compressed, value_weight, preferred_element_type=jnp.float32).astype(
        jnp.bfloat16
    )
    keys_all = jnp.concatenate([key_nope, latent[:, latent_width:]], axis=1)
    per_group = math.gcd(block_count, max(1, 512 // block_rows))
    group_count = block_count // per_group
    key_tiles = keys_all.reshape(block_count, block_rows, query_width)
    value_tiles = values.reshape(block_count, block_rows, value_width)
    causal = lax.broadcasted_iota(jnp.int32, (block_rows, block_rows), 0) >= lax.broadcasted_iota(
        jnp.int32, (block_rows, block_rows), 1
    )
    slot_range = jnp.arange(slot_count, dtype=jnp.int32)
    within = jnp.arange(per_group, dtype=jnp.int32)

    def one_group(carry, inputs):
        key_total, value_total = carry
        query_tile, grad_tile, group_slots, group_counts, group_index = inputs
        own_blocks = group_index * per_group + within
        keys_here = key_tiles[group_slots].reshape(per_group, slot_count * block_rows, query_width)
        values_here = value_tiles[group_slots].reshape(
            per_group, slot_count * block_rows, value_width
        )
        live = slot_range[None, :] < group_counts[:, None]
        diagonal = group_slots == own_blocks[:, None]
        allowed = live[:, None, :, None] & (
            jnp.logical_not(diagonal)[:, None, :, None] | causal[None, :, None, :]
        )
        allowed = allowed.reshape(per_group, block_rows, slot_count * block_rows)
        scores = (
            jnp.einsum("gqd,gkd->gqk", query_tile, keys_here, preferred_element_type=jnp.float32)
            * factor
        )
        scores = jnp.where(allowed, scores, -1e30)
        top_score = jnp.max(scores, axis=2, keepdims=True)
        expo = jnp.where(allowed, jnp.exp(scores - top_score), 0.0)
        probs = expo / jnp.sum(expo, axis=2, keepdims=True)
        probs_b = probs.astype(jnp.bfloat16)
        attended = jnp.einsum(
            "gqk,gkd->gqd", probs_b, values_here, preferred_element_type=jnp.float32
        )
        delta = jnp.sum(grad_tile.astype(jnp.float32) * attended, axis=2, keepdims=True)
        grad_probs = jnp.einsum(
            "gqd,gkd->gqk", grad_tile, values_here, preferred_element_type=jnp.float32
        )
        grad_scores = (probs * (grad_probs - delta)).astype(jnp.bfloat16)
        grad_query = (
            jnp.einsum("gqk,gkd->gqd", grad_scores, keys_here, preferred_element_type=jnp.float32)
            * factor
        ).astype(jnp.bfloat16)
        grad_key = (
            jnp.einsum("gqk,gqd->gkd", grad_scores, query_tile, preferred_element_type=jnp.float32)
            * factor
        )
        grad_value = jnp.einsum(
            "gqk,gqd->gkd", probs_b, grad_tile, preferred_element_type=jnp.float32
        )
        flat_slots = group_slots.reshape(per_group * slot_count)
        key_total = key_total.at[flat_slots].add(
            grad_key.reshape(per_group * slot_count, block_rows, query_width)
        )
        value_total = value_total.at[flat_slots].add(
            grad_value.reshape(per_group * slot_count, block_rows, value_width)
        )
        return ((key_total, value_total), grad_query)

    start = (
        jnp.zeros((block_count, block_rows, query_width), jnp.float32),
        jnp.zeros((block_count, block_rows, value_width), jnp.float32),
    )
    inputs = (
        head_queries.reshape(group_count, per_group, block_rows, query_width),
        head_grads.reshape(group_count, per_group, block_rows, value_width),
        slot_list.reshape(group_count, per_group, slot_count),
        count_list.reshape(group_count, per_group),
        jnp.arange(group_count, dtype=jnp.int32),
    )
    (key_total, value_total), grad_tiles = lax.scan(one_group, start, inputs)
    grad_query = grad_tiles.reshape(length, query_width)
    key_grads = key_total.reshape(length, query_width)
    nope_grads = key_grads[:, :nope_width].astype(jnp.bfloat16)
    value_grads = value_total.reshape(length, value_width).astype(jnp.bfloat16)
    latent_grad = jnp.dot(nope_grads, key_weight, preferred_element_type=jnp.float32) + jnp.einsum(
        "tv,lv->tl", value_grads, value_weight, preferred_element_type=jnp.float32
    )
    head_part = jnp.concatenate([latent_grad, key_grads[:, nope_width:]], axis=1).astype(
        jnp.bfloat16
    )
    key_weight_grad = jnp.einsum(
        "td,tl->dl", nope_grads, compressed, preferred_element_type=jnp.float32
    )
    value_weight_grad = jnp.einsum(
        "tl,tv->lv", compressed, value_grads, preferred_element_type=jnp.float32
    )
    return (grad_query, head_part, key_weight_grad, value_weight_grad)


def local(queries, grad_out, latent_kv, key_up, value_up, key_blocks, block_counts):
    head_queries, head_grads = (
        lax.all_to_all(queries, "seq", split_axis=2, concat_axis=1, tiled=True),
        lax.all_to_all(grad_out, "seq", split_axis=2, concat_axis=1, tiled=True),
    )
    latent = lax.all_gather(latent_kv, "seq", axis=1, tiled=True)[0]
    slot_list = key_blocks[0]
    count_list = block_counts[0]
    query_stack = jnp.moveaxis(head_queries[0], 1, 0)
    grad_stack = jnp.moveaxis(head_grads[0], 1, 0)

    def one_head(carry, inputs):
        head_q, head_g, key_weight, value_weight = inputs
        results = head_backward(
            head_q, head_g, latent, key_weight, value_weight, slot_list, count_list, BLK
        )
        return (carry, results)

    unused, (query_grads, head_parts, key_grads, value_grads) = lax.scan(
        one_head,
        jnp.zeros((), jnp.float32),
        (query_stack, grad_stack, key_up[:, 0], value_up[:, 0]),
    )
    returning = jnp.moveaxis(query_grads, 0, 1)[None]
    grad_queries = lax.all_to_all(returning, "seq", split_axis=1, concat_axis=2, tiled=True)
    heads_here, length, part_width = head_parts.shape
    seq_count = lax.axis_size("seq")
    tokens_here = length // seq_count
    pieces = head_parts.reshape(heads_here, seq_count, tokens_here, part_width)
    arrived = lax.all_to_all(pieces, "seq", split_axis=1, concat_axis=1, tiled=True)
    summed = jnp.sum(arrived.astype(jnp.float32), axis=(0, 1))
    grad_latent = lax.psum_scatter(summed, "sub", scatter_dimension=1, tiled=True)
    key_grads = key_grads[:, None]
    value_grads = value_grads[:, None]
    total_key, total_value = lax.psum((key_grads, value_grads), "rep")
    replica_count = lax.axis_size("rep")
    replica_index = lax.axis_index("rep")
    key_rows = total_key.shape[2] // replica_count
    value_rows = total_value.shape[2] // replica_count
    grad_key_up = lax.dynamic_slice_in_dim(total_key, replica_index * key_rows, key_rows, 2)
    grad_value_up = lax.dynamic_slice_in_dim(total_value, replica_index * value_rows, value_rows, 2)
    return (grad_queries, grad_latent[None], grad_key_up, grad_value_up)


def solution(mesh):
    placed = (
        P(("groups", "rep"), "seq", None, "sub"),
        P(("groups", "rep"), "seq", None, "sub"),
        P(("groups", "rep"), "seq", None),
        P("seq", "sub", None, None),
        P("seq", "sub", None, None),
        P(("groups", "rep"), None, None),
        P(("groups", "rep"), None),
    )
    return jax.shard_map(
        local,
        mesh=mesh,
        in_specs=placed,
        out_specs=(
            P(("groups", "rep"), "seq", None, "sub"),
            P(("groups", "rep"), "seq", "sub"),
            P(("groups", "seq"), "sub", "rep", None),
            P(("groups", "seq"), "sub", "rep", None),
        ),
        check_vma=False,
    )
```

profile of v0, /device:TPU:0, one launch (start us, length us, event | category | flops | bytes accessed | tf_op | source)
XLA Modules:
  0.0 474.2 jit_solution(6022909015443279409)
XLA Ops:
  8.0 1.6 copy.91
  9.6 31.8 %all_to_all.53 = bf16[1,128,32,128]{3,1,0,2:T(8,128)(2,1)S(1)} all-to-all(bf16[1,128,32,128]{3,1,0,2:T(8,128)(2,1)S(1)} %copy.91), channel_id=1, replica_groups=mesh['groups'=2,'seq'=4,'rep'=2,'sub'=2] {'seq'}, dimensions={2} | all-to-all | bytes 2097152 | tf_op jit(solution)/shard_map/all_to_all | solution.py:125
  41.5 3.7 all-to-all-start
  45.4 47.7 %all_gather.3 = bf16[1,512,576]{1,2,0:T(8,128)(2,1)S(1)} all-gather(bf16[1,128,576]{1,2,0:T(8,128)(2,1)S(1)} %copy-done.9), channel_id=1, replica_groups=mesh['groups'=2,'seq'=4,'rep'=2,'sub'=2] {'seq'}, dimensions={1}, use_global_device_ids=true | all-gather | bytes 737280 | tf_op jit(solution)/shard_map/all_gather | solution.py:127
  94.1 2.4 copy.90
  96.5 3.7 squeeze.63
  100.1 196.3 %while.18 = (s32[]{:T(128)}, bf16[8,512,192]{1,2,0:T(8,128)(2,1)}, bf16[8,512,576]{1,2,0:T(8,128)(2,1)}, f32[8,128,512]{2,1,0:T(8,128)}, f32[8,512,128]{2,1,0:T(...) while((s32[]{:T(128)}, bf16[8,512,192]{1,2,0:T(8,128)(2,1)}, ...), condition=%wide.wide.region_6.7_spmd, body=%wide.wide.region_0.6_spmd.sunk | while | flops 788646656 | bytes 57823416 | solution.py:140
  100.1 1.2 fusion.164
  112.0 1.8 scatter_fusion
  113.8 1.2 fusion.172
  115.0 2.6 fusion.173
  117.6 1.4 scatter_fusion.1
  119.0 1.3 fusion.174
  124.7 1.2 fusion.164
  136.5 1.8 scatter_fusion
  138.3 1.2 fusion.172
  139.5 2.6 fusion.173
  142.1 1.4 scatter_fusion.1
  143.6 1.3 fusion.174
  149.2 1.2 fusion.164
  161.0 1.8 scatter_fusion
  162.8 1.2 fusion.172
  164.0 2.6 fusion.173
  166.6 1.4 scatter_fusion.1
  168.1 1.3 fusion.174
  173.7 1.2 fusion.164
  185.5 1.8 scatter_fusion
  187.3 1.2 fusion.172
  188.6 2.6 fusion.173
  191.2 1.4 scatter_fusion.1
  192.6 1.3 fusion.174
  198.3 1.2 fusion.164
  210.1 1.8 scatter_fusion
  211.9 1.2 fusion.172
  213.2 2.6 fusion.173
  215.8 1.4 scatter_fusion.1
  217.2 1.3 fusion.174
  222.8 1.2 fusion.164
  234.6 1.8 scatter_fusion
  236.4 1.2 fusion.172
  237.7 2.6 fusion.173
  240.3 1.4 scatter_fusion.1
  241.7 1.3 fusion.174
  247.4 1.2 fusion.164
  259.2 1.8 scatter_fusion
  261.0 1.2 fusion.172
  262.2 2.6 fusion.173
  264.8 1.4 scatter_fusion.1
  266.3 1.3 fusion.174
  271.9 1.2 fusion.164
  283.7 1.8 scatter_fusion
  285.5 1.2 fusion.172
  286.8 2.6 fusion.173
  289.4 1.4 scatter_fusion.1
  290.8 1.3 fusion.174
  296.4 5.8 %copy_bitcast_fusion.2 = bf16[8,4,128,576]{2,3,0,1:T(8,128)(2,1)} fusion(bf16[8,512,576]{1,2,0:T(8,128)(2,1)} %get-tuple-element.196), kind=kLoop, calls=%fused_computation.76 | loop fusion | bytes 9437184 | tf_op jit(solution)/shard_map/reshape | solution.py:150
  302.2 6.3 %all-to-all-start.3 = ((bf16[8,4,128,576]{2,3,0,1:T(8,128)(2,1)}), bf16[8,4,128,576]{2,3,0,1:T(8,128)(2,1)}, u32[]{:S(2)}, u32[]{:S(2)}) async-start(bf16[8,4,128,576]{2,3,0,1:T(8,128)(2,1)} %copy_bitcast_fusion.2), calls=%async_computation.3 | async-start | bytes 9437184 | tf_op jit(solution)/shard_map/all_to_all | solution.py:151
  309.9 3.0 copy.94
  313.0 96.3 %all-to-all-done.3 = bf16[8,4,128,576]{2,3,0,1:T(8,128)(2,1)} async-done(((bf16[8,4,128,576]{2,3,0,1:T(8,128)(2,1)}), bf16[8,4,128,576]{2,3,0,1:T(8,128)(2,1)}, u32[]{:S(2)}, u32[]{:S(2)}) %all-to-all-start.3) | async-done | bytes 4718624 | tf_op jit(solution)/shard_map/all_to_all | solution.py:151
  409.2 3.6 all-to-all-start.2
  412.9 3.7 convert_reduce_fusion
  416.7 43.8 %all-to-all-done.2 = bf16[1,512,8,192]{3,2,0,1:T(8,128)(2,1)S(1)} async-done(((bf16[1,512,8,192]{3,2,0,1:T(8,128)(2,1)}), bf16[1,512,8,192]{3,2,0,1:T(8,128)(2,1)S(1)}, u32[]{:S(2)}, u32[]{:S(2)}) %all-to-all-start.2) | async-done | bytes 1572896 | tf_op jit(solution)/shard_map/all_to_all | solution.py:146
  460.5 2.8 copy.95
  463.3 2.4 constant_dynamic-slice_fusion.2
  (505 shorter events, 121.5 us)
Async XLA Ops:
  41.5 3.7 copy-start.10
  41.5 3.9 copy-start.9
  41.5 52.6 %all-to-all-start = ((bf16[1,128,32,192]{1,3,0,2:T(8,128)(2,1)}), bf16[1,128,32,192]{1,3,0,2:T(8,128)(2,1)S(1)}, u32[]{:S(2)}, u32[]{:S(2)}) async-start(bf16[1,128,32,192]{1,3,0,2:T(8,128)(2,1)} %bitcast.235), calls=%async_computation | async-start | bytes 3145728 | tf_op jit(solution)/shard_map/all_to_all | solution.py:124
  96.5 3.7 copy-start.11
  100.1 5.5 %copy-start = (bf16[512,576]{0,1:T(8,128)(2,1)}, bf16[512,576]{0,1:T(8,128)(2,1)S(1)}, u32[]{:S(2)}) copy-start(bf16[512,576]{0,1:T(8,128)(2,1)S(1)} %get-tuple-element.455) | copy-start | bytes 1769476 | tf_op jit(solution)/shard_map/while
  103.3 1.6 copy-start.3
  105.3 4.3 copy-start.2
  109.9 1.6 copy-start.5
  119.0 2.2 copy-start.1
  120.3 3.1 copy-start.4
  120.3 3.0 copy-start.6
  124.7 5.5 %copy-start = (bf16[512,576]{0,1:T(8,128)(2,1)}, bf16[512,576]{0,1:T(8,128)(2,1)S(1)}, u32[]{:S(2)}) copy-start(bf16[512,576]{0,1:T(8,128)(2,1)S(1)} %get-tuple-element.455) | copy-start | bytes 1769476 | tf_op jit(solution)/shard_map/while
  127.8 1.6 copy-start.3
  129.8 4.3 copy-start.2
  134.4 1.6 copy-start.5
  143.6 2.2 copy-start.1
  144.8 3.1 copy-start.4
  144.8 3.1 copy-start.6
  149.2 5.5 %copy-start = (bf16[512,576]{0,1:T(8,128)(2,1)}, bf16[512,576]{0,1:T(8,128)(2,1)S(1)}, u32[]{:S(2)}) copy-start(bf16[512,576]{0,1:T(8,128)(2,1)S(1)} %get-tuple-element.455) | copy-start | bytes 1769476 | tf_op jit(solution)/shard_map/while
  152.3 1.6 copy-start.3
  154.3 4.3 copy-start.2
  159.0 1.6 copy-start.5
  168.1 2.2 copy-start.1
  169.3 3.1 copy-start.4
  169.4 3.1 copy-start.6
  173.7 5.5 %copy-start = (bf16[512,576]{0,1:T(8,128)(2,1)}, bf16[512,576]{0,1:T(8,128)(2,1)S(1)}, u32[]{:S(2)}) copy-start(bf16[512,576]{0,1:T(8,128)(2,1)S(1)} %get-tuple-element.455) | copy-start | bytes 1769476 | tf_op jit(solution)/shard_map/while
  176.9 1.6 copy-start.3
  178.9 4.3 copy-start.2
  183.5 1.6 copy-start.5
  192.6 2.2 copy-start.1
  193.9 3.1 copy-start.4
  193.9 3.1 copy-start.6
  198.3 5.5 %copy-start = (bf16[512,576]{0,1:T(8,128)(2,1)}, bf16[512,576]{0,1:T(8,128)(2,1)S(1)}, u32[]{:S(2)}) copy-start(bf16[512,576]{0,1:T(8,128)(2,1)S(1)} %get-tuple-element.455) | copy-start | bytes 1769476 | tf_op jit(solution)/shard_map/while
  201.4 1.6 copy-start.3
  203.4 4.3 copy-start.2
  208.1 1.6 copy-start.5
  217.2 2.2 copy-start.1
  218.5 3.1 copy-start.4
  218.5 3.1 copy-start.6
  222.8 5.5 %copy-start = (bf16[512,576]{0,1:T(8,128)(2,1)}, bf16[512,576]{0,1:T(8,128)(2,1)S(1)}, u32[]{:S(2)}) copy-start(bf16[512,576]{0,1:T(8,128)(2,1)S(1)} %get-tuple-element.455) | copy-start | bytes 1769476 | tf_op jit(solution)/shard_map/while
  226.0 1.6 copy-start.3
  228.0 4.3 copy-start.2
  232.6 1.6 copy-start.5
  241.7 2.2 copy-start.1
  243.0 3.1 copy-start.4
  243.0 3.1 copy-start.6
  247.4 5.5 %copy-start = (bf16[512,576]{0,1:T(8,128)(2,1)}, bf16[512,576]{0,1:T(8,128)(2,1)S(1)}, u32[]{:S(2)}) copy-start(bf16[512,576]{0,1:T(8,128)(2,1)S(1)} %get-tuple-element.455) | copy-start | bytes 1769476 | tf_op jit(solution)/shard_map/while
  250.5 1.6 copy-start.3
  252.5 4.3 copy-start.2
  257.1 1.6 copy-start.5
  266.3 2.2 copy-start.1
  267.5 3.1 copy-start.4
  267.5 3.1 copy-start.6
  271.9 5.5 %copy-start = (bf16[512,576]{0,1:T(8,128)(2,1)}, bf16[512,576]{0,1:T(8,128)(2,1)S(1)}, u32[]{:S(2)}) copy-start(bf16[512,576]{0,1:T(8,128)(2,1)S(1)} %get-tuple-element.455) | copy-start | bytes 1769476 | tf_op jit(solution)/shard_map/while
  275.0 1.6 copy-start.3
  277.1 4.3 copy-start.2
  290.8 2.2 copy-start.1
  292.1 3.1 copy-start.4
  292.1 3.1 copy-start.6
  302.2 107.0 %all-to-all-start.3 = ((bf16[8,4,128,576]{2,3,0,1:T(8,128)(2,1)}), bf16[8,4,128,576]{2,3,0,1:T(8,128)(2,1)}, u32[]{:S(2)}, u32[]{:S(2)}) async-start(bf16[8,4,128,576]{2,3,0,1:T(8,128)(2,1)} %copy_bitcast_fusion.2), calls=%async_computation.3 | async-start | bytes 9437184 | tf_op jit(solution)/shard_map/all_to_all | solution.py:151
  308.5 154.8 %all-reduce.3.cloned.1.call-start = ((), (), s32[]{:S(2)}) async-start(), calls=%async_computation.6 | async-start | bytes 8388608 | tf_op jit(solution)/shard_map/psum | solution.py:156
  409.2 51.2 %all-to-all-start.2 = ((bf16[1,512,8,192]{3,2,0,1:T(8,128)(2,1)}), bf16[1,512,8,192]{3,2,0,1:T(8,128)(2,1)S(1)}, u32[]{:S(2)}, u32[]{:S(2)}) async-start(bf16[1,512,8,192]{3,2,0,1:T(8,128)(2,1)} %bitcast.33), calls=%async_computation.2 | async-start | bytes 4194304 | tf_op jit(solution)/shard_map/all_to_all | solution.py:146
  412.8 53.9 %reduce-scatter.2.cloned.1.call-start = ((), (), s32[]{:S(2)}) async-start(), calls=%async_computation.5 | async-start | bytes 442368 | tf_op jit(solution)/shard_map/reduce_scatter | solution.py:153
  463.3 2.4 copy-start.8
  (2 other events, 3.0 us)
Sparse Core Ops, SparseCore 0:
  311.8 109.7 all-reduce.2
Sparse Core Ops, SparseCore 1:
  416.7 9.0 reduce-scatter.1
where the time goes:
time: 476 us; the launch traced here: 474 us
  waiting for transfers between devices  141 us (30%)
  local copies, waits for them, and re-layouts  92.8 us (19%)
  matrix products  89.5 us (19%)
  blocking collectives  79.5 us (17%)
  other arithmetic  39.7 us (8%)
  between operations  15.5 us (3%)
  starting transfers between devices  13.6 us (3%)
    all_to_all x1, waiting for transfers between devices, local(): lax.all_to_all(pieces, 'seq', split_axis=1, concat_axis=1, tiled=True)  96.3 us
    all_gather x1, blocking collectives, local(): latent = lax.all_gather(latent_kv, 'seq', axis=1, tiled=True)[0]  47.7 us
    all_to_all x1, waiting for transfers between devices, local(): lax.all_to_all(returning, 'seq', split_axis=1, concat_axis=2, tiled=True)  43.8 us
    all_to_all x1, blocking collectives, local(): lax.all_to_all(grad_out, 'seq', split_axis=2, concat_axis=1, tiled=True)  31.8 us
    dot_general x8, matrix products, one_group(): jnp.einsum('gqk,gqd->gkd', probs_b, grad_tile, preferred_element_type=jnp...  20.5 us
    dynamic_slice x16, local copies, waits for them, and re-layouts, local(): lax.scan(one_head, jnp.zeros((), jnp.float32), (query_stack, grad_stack,...  16.6 us
    scatter-add x8, other arithmetic, one_group(): key_total.at[flat_slots]  14.2 us
    dynamic_update_slice x24, local copies, waits for them, and re-layouts, local(): lax.scan(one_head, jnp.zeros((), jnp.float32), (query_stack, grad_stack,...  12.4 us
  transfers between devices with their start and end apart: 5, of which 2 were waited for; matrix products, arithmetic and copies ran while one was open for 3% of the time, Pallas kernels for 0%

commit v1 on v0

--- a/solution.py
+++ b/solution.py
@@ -1,11 +1,178 @@
+import functools
 import math
 
 import jax
 import jax.numpy as jnp
 from jax import lax
+from jax.experimental import pallas as pl
+from jax.experimental.pallas import tpu as pltpu
 from jax.sharding import PartitionSpec as P
 
 BLK = 128
+NN = (((1,), (0,)), ((), ()))
+NT = (((1,), (1,)), ((), ()))
+
+
+def mm(a, b, dims=NN):
+    return lax.dot_general(a, b, dims, preferred_element_type=jnp.float32)
+
+
+def head_math(q_of, g_of, k_w, v_w, lat_t, lat, bias, keys, keys_t, dk, dv, blocks, store_dq):
+    nope = k_w.shape[0]
+    width = k_w.shape[1]
+    total = lat_t.shape[1]
+    query_width = keys_t.shape[0]
+    factor = 1.0 / math.sqrt(query_width)
+    keys[:, :nope] = mm(lat[:, :width], k_w, NT).astype(jnp.bfloat16)
+    keys_t[:nope, :] = mm(k_w, lat_t[:width, :]).astype(jnp.bfloat16)
+    values = mm(lat[:, :width], v_w).astype(jnp.bfloat16)
+    for pair in reversed(range(blocks // 2)):
+        seen = (2 * pair + 2) * BLK
+        q2 = jnp.concatenate([q_of(2 * pair), q_of(2 * pair + 1)], axis=1)
+        g2 = jnp.concatenate([g_of(2 * pair), g_of(2 * pair + 1)], axis=1)
+        scores = mm(keys[:seen, :query_width], q2) * factor
+        scores = scores + bias[:seen, 2 * pair * BLK : seen]
+        expo = jnp.exp(scores - jnp.max(scores, axis=0, keepdims=True))
+        probs = expo * (1.0 / jnp.sum(expo, axis=0, keepdims=True))
+        probs_b = probs.astype(jnp.bfloat16)
+        grad_probs = mm(values[:seen], g2)
+        delta = jnp.sum(probs_b.astype(jnp.float32) * grad_probs, axis=0, keepdims=True)
+        grad_scores = (probs * (grad_probs - delta)).astype(jnp.bfloat16)
+        dq = (mm(keys_t[:, :seen], grad_scores) * factor).astype(jnp.bfloat16)
+        store_dq(2 * pair, dq[:, :BLK])
+        store_dq(2 * pair + 1, dq[:, BLK:])
+        dk_part = mm(q2, grad_scores, NT)
+        dv_part = mm(g2, probs_b, NT)
+        if seen == total:
+            dk[...] = dk_part
+            dv[...] = dv_part
+        else:
+            dk[:, :seen] += dk_part
+            dv[:, :seen] += dv_part
+    nope_b = (dk[:nope, :] * factor).astype(jnp.bfloat16)
+    rope = dk[nope:, :] * factor
+    value_b = dv[...].astype(jnp.bfloat16)
+    latent_part = mm(k_w.T, nope_b) + mm(v_w, value_b)
+    k_grad = mm(nope_b, lat_t[:width, :], NT)
+    v_grad = mm(lat_t[:width, :], value_b, NT)
+    return latent_part, rope, k_grad, v_grad
+
+
+def block_bias(slots, counts, blocks):
+    live = jnp.arange(slots.shape[1], dtype=jnp.int32)[None, :] < counts[:, None]
+    blocks_here = jnp.arange(blocks, dtype=jnp.int32)
+    listed = jnp.any((slots[None] == blocks_here[:, None, None]) & live[None], axis=2)
+    position = jnp.arange(blocks * BLK, dtype=jnp.int32)
+    wide = jnp.repeat(jnp.repeat(listed, BLK, axis=0), BLK, axis=1)
+    allowed = wide & (position[:, None] <= position[None, :])
+    return jnp.where(allowed, 0.0, -1e30).astype(jnp.float32)
+
+
+def attention_kernel(
+    blocks, q_ref, g_ref, lat_t, bias, k_ref, v_ref, dq_ref, dlat_ref, dk_ref, dv_ref,
+    lat, keys, keys_t, dk, dv
+):
+    width = k_ref.shape[2]
+    nope = k_ref.shape[1]
+
+    @pl.when(pl.program_id(0) == 0)
+    def _():
+        dlat_ref[...] = jnp.zeros_like(dlat_ref)
+        lat[...] = lat_t[:width, :].T
+        keys[:, nope : keys_t.shape[0]] = lat_t[width:, :].T
+        keys_t[nope:, :] = lat_t[width:, :]
+
+    def store_dq(block, value):
+        dq_ref[block, 0] = value
+
+    latent_part, rope, k_grad, v_grad = head_math(
+        lambda b: q_ref[b, 0], lambda b: g_ref[b, 0], k_ref[0], v_ref[0], lat_t, lat, bias,
+        keys, keys_t, dk, dv, blocks, store_dq
+    )
+    dlat_ref[:width, :] += latent_part
+    dlat_ref[width:, :] += rope
+    dk_ref[0] = k_grad
+    dv_ref[0] = v_grad
+
+
+def attention_call(q_all, g_all, lat_t, bias, k_w, v_w):
+    blocks, heads, query_width, _ = q_all.shape
+    value_width = g_all.shape[2]
+    kv_width, total = lat_t.shape
+    nope, width = k_w.shape[1:]
+    whole = lambda *shape: pl.BlockSpec(shape, lambda h: (0,) * len(shape))
+    return pl.pallas_call(
+        functools.partial(attention_kernel, blocks),
+        grid=(heads,),
+        in_specs=[
+            pl.BlockSpec((blocks, 1, query_width, BLK), lambda h: (0, h, 0, 0)),
+            pl.BlockSpec((blocks, 1, value_width, BLK), lambda h: (0, h, 0, 0)),
+            whole(kv_width, total),
+            whole(total, total),
+            pl.BlockSpec((1, nope, width), lambda h: (h, 0, 0)),
+            pl.BlockSpec((1, width, value_width), lambda h: (h, 0, 0)),
+        ],
+        out_specs=[
+            pl.BlockSpec((blocks, 1, query_width, BLK), lambda h: (0, h, 0, 0)),
+            whole(kv_width, total),
+            pl.BlockSpec((1, nope, width), lambda h: (h, 0, 0)),
+            pl.BlockSpec((1, width, value_width), lambda h: (h, 0, 0)),
+        ],
+        out_shape=[
+            jax.ShapeDtypeStruct(q_all.shape, jnp.bfloat16),
+            jax.ShapeDtypeStruct((kv_width, total), jnp.float32),
+            jax.ShapeDtypeStruct(k_w.shape, jnp.float32),
+            jax.ShapeDtypeStruct(v_w.shape, jnp.float32),
+        ],
+        scratch_shapes=[
+            pltpu.VMEM((total, width), jnp.bfloat16),
+            pltpu.VMEM((total, 2 * BLK), jnp.bfloat16),
+            pltpu.VMEM((query_width, total), jnp.bfloat16),
+            pltpu.VMEM((query_width, total), jnp.float32),
+            pltpu.VMEM((value_width, total), jnp.float32),
+        ],
+        compiler_params=pltpu.CompilerParams(
+            dimension_semantics=("arbitrary",), vmem_limit_bytes=40 << 20
+        ),
+    )(q_all, g_all, lat_t, bias, k_w, v_w)
+
+
+def halves_exchange(grads, dim):
+    rows = grads.shape[dim] // 2
+    index = lax.axis_index("rep")
+    mine = lax.dynamic_slice_in_dim(grads, index * rows, rows, dim)
+    other = lax.dynamic_slice_in_dim(grads, (1 - index) * rows, rows, dim).astype(jnp.bfloat16)
+    return mine + lax.ppermute(other, "rep", [(0, 1), (1, 0)]).astype(jnp.float32)
+
+
+def local_small(queries, grad_out, latent_kv, key_up, value_up, key_blocks, block_counts):
+    shards = lax.axis_size("seq")
+    heads = key_up.shape[0]
+    tokens = queries.shape[1]
+    q_t = jnp.transpose(queries[0], (1, 2, 0))
+    g_t = jnp.transpose(grad_out[0], (1, 2, 0))
+    lat_t = lax.all_gather(latent_kv[0].T, "seq", axis=1, tiled=True)
+    q_all = lax.all_to_all(q_t, "seq", split_axis=0, concat_axis=0, tiled=True)
+    g_all = lax.all_to_all(g_t, "seq", split_axis=0, concat_axis=0, tiled=True)
+    q_all = q_all.reshape(shards, heads, q_t.shape[1], tokens)
+    g_all = g_all.reshape(shards, heads, g_t.shape[1], tokens)
+    bias = block_bias(key_blocks[0], block_counts[0], shards)
+    dq, dlat, dk, dv = attention_call(
+        q_all, g_all, lat_t, bias, key_up[:, 0], value_up[:, 0]
+    )
+    returned = lax.all_to_all(
+        dq.reshape(shards * heads, q_t.shape[1], tokens), "seq", split_axis=0, concat_axis=0,
+        tiled=True
+    )
+    grad_queries = jnp.transpose(returned, (2, 0, 1))[None]
+    half = lax.psum_scatter(dlat, "sub", scatter_dimension=0, tiled=True)
+    grad_latent = lax.psum_scatter(half, "seq", scatter_dimension=1, tiled=True)
+    return (
+        grad_queries,
+        grad_latent.T[None],
+        halves_exchange(dk[:, None], 2),
+        halves_exchange(dv[:, None], 2),
+    )
 
 
 def head_backward(
@@ -119,7 +286,7 @@
     return (grad_query, head_part, key_weight_grad, value_weight_grad)
 
 
-def local(queries, grad_out, latent_kv, key_up, value_up, key_blocks, block_counts):
+def local_general(queries, grad_out, latent_kv, key_up, value_up, key_blocks, block_counts):
     head_queries, head_grads = (
         lax.all_to_all(queries, "seq", split_axis=2, concat_axis=1, tiled=True),
         lax.all_to_all(grad_out, "seq", split_axis=2, concat_axis=1, tiled=True),
@@ -173,6 +340,18 @@
         P(("groups", "rep"), None, None),
         P(("groups", "rep"), None),
     )
+
+    def local(queries, grad_out, latent_kv, key_up, value_up, key_blocks, block_counts):
+        args = (queries, grad_out, latent_kv, key_up, value_up, key_blocks, block_counts)
+        shards = mesh.shape["seq"]
+        small = (
+            queries.shape[1] == BLK
+            and shards % 2 == 0
+            and shards * BLK <= 1024
+            and mesh.shape["rep"] == 2
+        )
+        return local_small(*args) if small else local_general(*args)
+
     return jax.shard_map(
         local,
         mesh=mesh,

time: 476 us -> 184 us (0.39)
  waiting for transfers between devices: 141 us -> 34.2 us
  matrix products: 89.5 us -> 0 us
  local copies, waits for them, and re-layouts: 92.8 us -> 18.1 us
  other arithmetic: 39.7 us -> 4.83 us
  Pallas kernels: 0 us -> 20.4 us
    all_to_all x3 -> x2, waiting for transfers between devices: 140 us -> 8.44 us  [the longest x1 8.44 us: local_small(): lax.all_to_all(dq.reshape(shards * heads, q_t.shape[1], tokens), 'seq', s...]
    dot_general x96 -> x0, matrix products: 89.5 us -> none  [the longest x8 20.5 us: one_group(): jnp.einsum('gqk,gqd->gkd', probs_b, grad_tile, preferred_element_type=jnp...]
    scatter-add x16 -> x0, other arithmetic: 25.2 us -> none  [the longest x8 14.2 us: one_group(): key_total.at[flat_slots]]
    ppermute x0 -> x2, waiting for transfers between devices: none -> 20.7 us  [halves_exchange(): lax.ppermute(other, 'rep', [(0, 1), (1, 0)]).astype(jnp.float32)]
    pallas_call x0 -> x1, Pallas kernels: none -> 20.4 us  [attention_call(): pl.pallas_call(functools.partial(attention_kernel, blocks), grid=(heads,)...]
    dynamic_slice x18 -> x0, local copies, waits for them, and re-layouts: 20.1 us -> none  [the longest x16 16.6 us: local(): lax.scan(one_head, jnp.zeros((), jnp.float32), (query_stack, grad_stack,...]
    reshape x34 -> x0, local copies, waits for them, and re-layouts: 17.2 us -> none  [the longest x16 6.84 us: one_group(): grad_key.reshape(per_group * slot_count, block_rows, query_width)]
    gather x24 -> x0, local copies, waits for them, and re-layouts: 13.6 us -> none  [the longest x16 8.55 us: one_group(): key_tiles[group_slots]]
  transfers between devices with their start and end apart: 5 -> 6, of which waited for: 2 -> 4; matrix products, arithmetic and copies ran while one was open for 3% -> 5% of each run, Pallas kernels for 0% -> 0%
where the time goes in v1:
time: 184 us
  blocking collectives  79.7 us (43%)
  waiting for transfers between devices  34.2 us (19%)
  Pallas kernels  20.4 us (11%)
  local copies, waits for them, and re-layouts  18.1 us (10%)
  between operations  14.2 us (8%)
  starting transfers between devices  12.3 us (7%)
  other arithmetic  4.83 us (3%)
    all_gather x1, blocking collectives, local_small(): lat_t = lax.all_gather(latent_kv[0].T, 'seq', axis=1, tiled=True)  47.8 us
    all_to_all x1, blocking collectives, local_small(): g_all = lax.all_to_all(g_t, 'seq', split_axis=0, concat_axis=0, tiled=True)  31.9 us
    ppermute x2, waiting for transfers between devices, halves_exchange(): lax.ppermute(other, 'rep', [(0, 1), (1, 0)]).astype(jnp.float32)  20.7 us
    pallas_call x1, Pallas kernels, attention_call(): pl.pallas_call(functools.partial(attention_kernel, blocks), grid=(heads,)...  20.4 us
    unnamed x24, local copies, waits for them, and re-layouts  12.8 us
    all_to_all x1, waiting for transfers between devices, local_small(): lax.all_to_all(dq.reshape(shards * heads, q_t.shape[1], tokens), 'seq', s...  8.44 us
    all_to_all x1, starting transfers between devices, local_small(): lax.all_to_all(dq.reshape(shards * heads, q_t.shape[1], tokens), 'seq', s...  6.42 us
    reduce_scatter x1, waiting for transfers between devices, local_small(): half = lax.psum_scatter(dlat, 'sub', scatter_dimension=0, tiled=True)  5.03 us
  transfers between devices with their start and end apart: 6, of which 4 were waited for; matrix products, arithmetic and copies ran while one was open for 5% of the time, Pallas kernels for 0%

profile of v1, /device:TPU:0, one launch (start us, length us, event | category | flops | bytes accessed | tf_op | source)
XLA Modules:
  0.0 183.7 jit_solution(4369196417620769717)
XLA Ops:
  7.2 1.6 copy.31
  8.8 31.9 %all_to_all.15 = bf16[32,128,128]{1,2,0:T(8,128)(2,1)} all-to-all(bf16[32,128,128]{1,2,0:T(8,128)(2,1)S(1)} %bitcast.52), channel_id=1, replica_groups=mesh['groups'=2,'seq'=4,'rep'=2,'sub'=2] {'seq'}, dimensions={0} | all-to-all | bytes 2097152 | tf_op jit(solution)/shard_map/all_to_all | solution.py:156
  40.7 0.0 copy-start.9
  40.8 0.0 copy-start.10
  40.8 0.0 copy-start.8
  40.8 3.7 %all-to-all-start = ((bf16[32,192,128]{2,1,0:T(8,128)(2,1)}), bf16[32,192,128]{2,1,0:T(8,128)(2,1)S(1)}, u32[]{:S(2)}, u32[]{:S(2)}) async-start(bf16[32,192,128]{2,1,0:T(8,128)(2,1)} %bitcast.1), calls=%async_computation | async-start | bytes 3145728 | tf_op jit(solution)/shard_map/all_to_all | solution.py:155
  44.5 0.0 reduce-scatter.3.cloned.1.call-start
  44.5 0.0 copy-done.9
  44.5 0.0 copy-done.10
  44.6 0.0 copy-done.8
  44.6 47.8 %all_gather.3.lat_t = bf16[576,512]{1,0:T(8,128)(2,1)S(1)} all-gather(bf16[576,128]{1,0:T(8,128)(2,1)S(1)} %bitcast.55), channel_id=1, replica_groups=mesh['groups'=2,'seq'=4,'rep'=2,'sub'=2] {'seq'}, dimensions={1}, use_global_device_ids=true | all-gather | bytes 737280 | tf_op jit(solution)/shard_map/all_gather | solution.py:154
  92.4 1.6 broadcast_in_dim.28
  94.0 0.2 fusion.3.bias
  94.1 2.3 %copy.21 = bf16[32,128,128]{2,1,0:T(8,128)(2,1)} copy(bf16[32,128,128]{1,2,0:T(8,128)(2,1)} %all_to_all.15) | data formatting | bytes 2097152 | tf_op jit(solution)/shard_map/all_to_all | solution.py:156
  96.4 0.0 all-to-all-done
  96.4 0.0 copy-start
  96.4 1.2 copy-done
  97.6 0.0 copy-start.6
  97.6 1.2 copy-done.6
  98.9 0.0 copy-start.7
  98.9 1.2 copy-done.7
  100.1 20.4 %shard_map.102 = (bf16[4,8,192,128]{3,2,1,0:T(8,128)(2,1)S(1)}, f32[576,512]{1,0:T(8,128)S(1)}, f32[8,128,512]{2,1,0:T(8,128)S(1)}, f32[8,512,128]{2,1,0:T(8,128)S(1)}) custom-call(bf16[4,8,192,128]{3,2,1,0:T(8,128)(2,1)S(1)} %bitcast.47, bf16[4,8,128,128]{3,2,1,0:T(8,128)(2,1)S(1)} %bitcast.48, bf16[576,512]{1,0:T(8,128)(2,1)S(1)} %all_gather.3.lat_t, ...), custom_call_target="tpu_custom_call" | custom-call | tf_op jit(solution)/shard_map/pallas_call | solution.py:104
  120.4 0.0 copy-start.1
  120.5 1.1 copy-done.1
  121.6 0.0 copy-start.2
  121.6 1.0 copy-done.2
  122.6 0.0 copy-start.3
  122.6 1.3 copy-done.3
  124.0 0.0 copy-start.5
  124.0 1.3 copy-done.5
  125.3 0.0 reduce-scatter.3.cloned.1.call-update
  125.3 0.0 copy-start.4
  125.3 6.4 %all-to-all-start.2 = ((bf16[32,192,128]{2,1,0:T(8,128)(2,1)}), bf16[32,192,128]{2,1,0:T(8,128)(2,1)}, u32[]{:S(2)}, u32[]{:S(2)}) async-start(bf16[32,192,128]{2,1,0:T(8,128)(2,1)} %bitcast.49), calls=%async_computation.2 | async-start | bytes 3145728 | tf_op jit(solution)/shard_map/all_to_all | solution.py:163
  131.7 0.0 reduce-scatter.5.cloned.1.call-start
  131.7 5.0 %reduce-scatter.3.cloned.1.call-done = f32[288,512]{1,0:T(8,128)} async-done(((f32[576,512]{1,0:T(8,128)}), f32[288,512]{1,0:T(8,128)}) %reduce-scatter.3.cloned.1.call-update) | async-done | bytes 589840 | tf_op jit(solution)/shard_map/reduce_scatter | solution.py:168
  136.8 0.0 reduce-scatter.5.cloned.1.call-update
  136.8 1.3 fusion.4
  138.1 1.8 collective-permute-start
  139.9 0.0 copy-done.4
  139.9 0.1 fusion.5
  140.0 0.3 collective-permute-start.1
  140.4 12.7 %collective-permute-done = bf16[8,1,64,512]{3,2,0,1:T(8,128)(2,1)} collective-permute-done((bf16[8,1,64,512]{3,2,0,1:T(8,128)(2,1)S(1)}, bf16[8,1,64,512]{3,2,0,1:T(8,128)(2,1)}, u32[]{:S(2)}, u32[]{:S(2)}) %collective-permute-start) | collective-permute-done | bytes 524320 | tf_op jit(solution)/shard_map/ppermute | solution.py:145
  153.0 2.5 %fusion.1 = f32[8,1,64,512]{3,2,1,0:T(8,128)} fusion(bf16[8,1,64,512]{3,2,0,1:T(8,128)(2,1)} %collective-permute-done, f32[8,128,512]{2,1,0:T(8,128)} %copy-done.5, s32[]{:T(128)S(6)} %select_n.17), kind=kLoop, calls=%fused_computation.3 | loop fusion | flops 524288 | bytes 2621444
  155.6 8.1 %collective-permute-done.1 = bf16[8,1,256,128]{3,2,0,1:T(8,128)(2,1)} collective-permute-done((bf16[8,1,256,128]{3,2,0,1:T(8,128)(2,1)S(1)}, bf16[8,1,256,128]{3,2,0,1:T(8,128)(2,1)}, u32[]{:S(2)}, u32[]{:S(2)}) %collective-permute-start.1) | collective-permute-done | bytes 524320 | tf_op jit(solution)/shard_map/ppermute | solution.py:145
  163.6 2.1 %fusion = f32[8,1,256,128]{3,2,1,0:T(8,128)} fusion(bf16[8,1,256,128]{3,2,0,1:T(8,128)(2,1)} %collective-permute-done.1, f32[8,512,128]{2,1,0:T(8,128)S(1)} %copy-done.4, s32[]{:T(128)S(6)} %select_n.19), kind=kLoop, calls=%fused_computation.1 | loop fusion | flops 524288 | bytes 2621444
  165.7 8.4 %all-to-all-done.2 = bf16[32,192,128]{2,1,0:T(8,128)(2,1)} async-done(((bf16[32,192,128]{2,1,0:T(8,128)(2,1)}), bf16[32,192,128]{2,1,0:T(8,128)(2,1)}, u32[]{:S(2)}, u32[]{:S(2)}) %all-to-all-start.2) | async-done | bytes 1572896 | tf_op jit(solution)/shard_map/all_to_all | solution.py:163
  174.2 0.0 reduce-scatter.5.cloned.1.call-done
  174.2 2.7 %copy.34 = bf16[1,128,32,192]{1,3,2,0:T(8,128)(2,1)} copy(bf16[1,128,32,192]{1,3,2,0:T(8,128)(2,1)} %bitcast.16) | data formatting | bytes 3145728
  (4 shorter events, 0.0 us)
Async XLA Ops:
  40.7 3.8 %copy-start.9 = (s32[1,4,3]{1,0,2:T(1,128)S(1)}, s32[1,4,3]{1,0,2:T(1,128)}, u32[]{:S(2)}) copy-start(s32[1,4,3]{1,0,2:T(1,128)} %param.12) | copy-start | bytes 148
  40.8 3.8 %copy-start.10 = (s32[1,4]{1,0:T(1,128)S(1)}, s32[1,4]{1,0:T(1,128)}, u32[]{:S(2)}) copy-start(s32[1,4]{1,0:T(1,128)} %param.13) | copy-start | bytes 52
  40.8 3.8 %copy-start.8 = (bf16[1,128,576]{1,2,0:T(8,128)(2,1)S(1)}, bf16[1,128,576]{1,2,0:T(8,128)(2,1)}, u32[]{:S(2)}) copy-start(bf16[1,128,576]{1,2,0:T(8,128)(2,1)} %param.9) | copy-start | bytes 442372
  40.8 55.7 %all-to-all-start = ((bf16[32,192,128]{2,1,0:T(8,128)(2,1)}), bf16[32,192,128]{2,1,0:T(8,128)(2,1)S(1)}, u32[]{:S(2)}, u32[]{:S(2)}) async-start(bf16[32,192,128]{2,1,0:T(8,128)(2,1)} %bitcast.1), calls=%async_computation | async-start | bytes 3145728 | tf_op jit(solution)/shard_map/all_to_all | solution.py:155
  44.5 92.3 %reduce-scatter.3.cloned.1.call-start = ((), (), s32[]{:S(2)}) async-start(), calls=%async_computation.5 | async-start | bytes 1769472 | tf_op jit(solution)/shard_map/reduce_scatter | solution.py:168
  96.4 1.2 copy-start
  97.6 1.2 copy-start.6
  98.9 1.2 copy-start.7
  120.4 1.1 copy-start.1
  121.6 1.0 copy-start.2
  122.6 1.3 copy-start.3
  124.0 1.3 copy-start.5
  125.3 14.6 %copy-start.4 = (f32[8,512,128]{2,1,0:T(8,128)S(1)}, f32[8,512,128]{2,1,0:T(8,128)}, u32[]{:S(2)}) copy-start(f32[8,512,128]{2,1,0:T(8,128)} %copy-done.3) | copy-start | bytes 6291460
  125.3 48.9 %all-to-all-start.2 = ((bf16[32,192,128]{2,1,0:T(8,128)(2,1)}), bf16[32,192,128]{2,1,0:T(8,128)(2,1)}, u32[]{:S(2)}, u32[]{:S(2)}) async-start(bf16[32,192,128]{2,1,0:T(8,128)(2,1)} %bitcast.49), calls=%async_computation.2 | async-start | bytes 3145728 | tf_op jit(solution)/shard_map/all_to_all | solution.py:163
  131.7 42.4 %reduce-scatter.5.cloned.1.call-start = ((), (), s32[]{:S(2)}) async-start(), calls=%async_computation.6 | async-start | bytes 737280 | tf_op jit(solution)/shard_map/reduce_scatter | solution.py:169
  138.1 14.9 %collective-permute-start = (bf16[8,1,64,512]{3,2,0,1:T(8,128)(2,1)S(1)}, bf16[8,1,64,512]{3,2,0,1:T(8,128)(2,1)}, u32[]{:S(2)}, u32[]{:S(2)}) collective-permute-start(bf16[8,1,64,512]{3,2,0,1:T(8,128)(2,1)S(1)} %fusion.4), channel_id=1, source_target_pairs={{0,2},{2,0},{1,3},{3,1},{4,6},{6,4},{5,7},{7,5},{8,10},{10,8},{9,1... | collective-permute-start | bytes 1572872 | tf_op jit(solution)/shard_map/ppermute | solution.py:145
  140.0 23.6 %collective-permute-start.1 = (bf16[8,1,256,128]{3,2,0,1:T(8,128)(2,1)S(1)}, bf16[8,1,256,128]{3,2,0,1:T(8,128)(2,1)}, u32[]{:S(2)}, u32[]{:S(2)}) collective-permute-start(bf16[8,1,256,128]{3,2,0,1:T(8,128)(2,1)S(1)} %fusion.5), channel_id=1, source_target_pairs={{0,2},{2,0},{1,3},{3,1},{4,6},{6,4},{5,7},{7,5},{8,10},{10,8},{9,1... | collective-permute-start | bytes 1572872 | tf_op jit(solution)/shard_map/ppermute | solution.py:145
Sparse Core Ops, SparseCore 0:
  125.4 11.2 reduce-scatter.2
  139.7 30.3 reduce-scatter.4

commit v2 on v0

--- a/solution.py
+++ b/solution.py
@@ -1,11 +1,324 @@
+import functools
 import math
 
 import jax
 import jax.numpy as jnp
 from jax import lax
+from jax.experimental import pallas as pl
+from jax.experimental.pallas import tpu as pltpu
 from jax.sharding import PartitionSpec as P
 
 BLK = 128
+NN = (((1,), (0,)), ((), ()))
+NT = (((1,), (1,)), ((), ()))
+
+
+def mm(a, b, dims=NN):
+    return lax.dot_general(a, b, dims, preferred_element_type=jnp.float32)
+
+
+def head_math(q_of, g_of, k_w, v_w, lat_t, lat, bias, keys, keys_t, dk, dv, blocks, store_dq):
+    nope = k_w.shape[0]
+    width = k_w.shape[1]
+    total = lat_t.shape[1]
+    query_width = keys_t.shape[0]
+    factor = 1.0 / math.sqrt(query_width)
+    keys[:, :nope] = mm(lat[...], k_w, NT).astype(jnp.bfloat16)
+    keys_t[:nope, :] = mm(k_w, lat_t[:width, :]).astype(jnp.bfloat16)
+    values = mm(lat[...], v_w).astype(jnp.bfloat16)
+    for pair in reversed(range(blocks // 2)):
+        seen = (2 * pair + 2) * BLK
+        q2 = jnp.concatenate([q_of(2 * pair), q_of(2 * pair + 1)], axis=1)
+        g2 = jnp.concatenate([g_of(2 * pair), g_of(2 * pair + 1)], axis=0)
+        scores = mm(keys[:seen, :query_width], q2) * factor
+        scores = scores + bias[:seen, 2 * pair * BLK : seen]
+        expo = jnp.exp(scores - jnp.max(scores, axis=0, keepdims=True))
+        probs = expo * (1.0 / jnp.sum(expo, axis=0, keepdims=True))
+        probs_b = probs.astype(jnp.bfloat16)
+        grad_probs = mm(values[:seen], g2, NT)
+        delta = jnp.sum(probs_b.astype(jnp.float32) * grad_probs, axis=0, keepdims=True)
+        grad_scores = (probs * (grad_probs - delta)).astype(jnp.bfloat16)
+        dq = (mm(keys_t[:, :seen], grad_scores) * factor).astype(jnp.bfloat16)
+        store_dq(2 * pair, dq[:, :BLK])
+        store_dq(2 * pair + 1, dq[:, BLK:])
+        dk_part = mm(q2, grad_scores, NT)
+        dv_part = mm(probs_b, g2)
+        if seen == total:
+            dk[...] = dk_part
+            dv[...] = dv_part
+        else:
+            dk[:, :seen] += dk_part
+            dv[:seen, :] += dv_part
+    nope_b = (dk[:nope, :] * factor).astype(jnp.bfloat16)
+    rope = dk[nope:, :] * factor
+    value_b = dv[...].astype(jnp.bfloat16)
+    latent_part = mm(k_w.T, nope_b) + mm(v_w, value_b, NT)
+    k_grad = mm(nope_b, lat_t[:width, :], NT)
+    v_grad = mm(lat_t[:width, :], value_b)
+    return latent_part, rope, k_grad, v_grad
+
+
+AHEAD = 4
+
+
+def attention_kernel(
+    shards, heads,
+    slots, counts, q_in, g_in, lat_in, k_in, v_in,
+    dq_out, lat_out, dk_out, dv_out,
+    q_buf, g_buf, lat_buf, k_w, v_w, dq_buf, lat_t, lat, bias, keys, keys_t, dk, dv, dlat,
+    k_half, v_half, kx_out, kx_in, vx_out, vx_in, half_in, piece_out, piece_in,
+    q_send, q_recv, g_send, g_recv, lat_send, lat_recv, dq_send, dq_recv, dq_local,
+    kx_sem, vx_sem, half_sem, piece_send, piece_recv, own_sem,
+):
+    me = lax.axis_index("seq")
+    rep = lax.axis_index("rep")
+    sub = lax.axis_index("sub")
+    kv_width, total = lat_t.shape
+    width = lat.shape[1]
+    nope = k_w.shape[1]
+    query_width = keys_t.shape[0]
+    k_rows = kx_in.shape[1]
+    v_rows = vx_in.shape[1]
+    half_rows = kv_width // 2
+    peers = range(1, shards)
+
+    def peer(d):
+        return lax.rem(me + d, shards)
+
+    def remote(src, dst, send, recv, axis, index):
+        return pltpu.make_async_remote_copy(
+            src_ref=src, dst_ref=dst, send_sem=send, recv_sem=recv,
+            device_id={axis: index}, device_id_type=pl.DeviceIdType.MESH,
+        )
+
+    def q_copy(d, h):
+        return remote(q_in.at[peer(d) * heads + h], q_buf.at[me, h],
+                      q_send.at[d - 1, h], q_recv.at[d - 1, h], "seq", peer(d))
+
+    def g_copy(d, h):
+        return remote(g_in.at[peer(d) * heads + h], g_buf.at[me, h],
+                      g_send.at[d - 1, h], g_recv.at[d - 1, h], "seq", peer(d))
+
+    def lat_copy(d):
+        return remote(lat_in, lat_buf.at[me], lat_send.at[d - 1], lat_recv.at[d - 1],
+                      "seq", peer(d))
+
+    def dq_copy(d, h):
+        return remote(dq_buf.at[peer(d), h], dq_out.at[me * heads + h],
+                      dq_send.at[d - 1, h], dq_recv.at[d - 1, h], "seq", peer(d))
+
+    def dq_own(h):
+        return pltpu.make_async_copy(
+            dq_buf.at[me, h], dq_out.at[me * heads + h], dq_local.at[h])
+
+    def k_copy(h):
+        return remote(kx_out.at[h], kx_in.at[h], kx_sem.at[0, h], kx_sem.at[1, h],
+                      "rep", 1 - rep)
+
+    def v_copy(h):
+        return remote(vx_out.at[h], vx_in.at[h], vx_sem.at[0, h], vx_sem.at[1, h],
+                      "rep", 1 - rep)
+
+    barrier = pltpu.get_barrier_semaphore()
+    for d in peers:
+        pl.semaphore_signal(barrier, inc=1, device_id={"seq": peer(d)},
+                            device_id_type=pl.DeviceIdType.MESH)
+    pl.semaphore_signal(barrier, inc=1, device_id={"rep": 1 - rep},
+                        device_id_type=pl.DeviceIdType.MESH)
+    pl.semaphore_signal(barrier, inc=1, device_id={"sub": 1 - sub},
+                        device_id_type=pl.DeviceIdType.MESH)
+    pl.semaphore_wait(barrier, shards + 1)
+
+    for d in peers:
+        lat_copy(d).start()
+
+    def send_head(h):
+        for d in peers:
+            q_copy(d, h).start()
+            g_copy(d, h).start()
+
+    def first(h, unused):
+        send_head(h)
+        return unused
+
+    lax.fori_loop(0, min(AHEAD, heads), first, 0)
+    own = pl.ds(me * heads, heads)
+    locals_ = [
+        pltpu.make_async_copy(lat_in, lat_buf.at[me], own_sem.at[0]),
+        pltpu.make_async_copy(q_in.at[own], q_buf.at[me], own_sem.at[1]),
+        pltpu.make_async_copy(g_in.at[own], g_buf.at[me], own_sem.at[2]),
+        pltpu.make_async_copy(k_in, k_w, own_sem.at[3]),
+        pltpu.make_async_copy(v_in, v_w, own_sem.at[4]),
+    ]
+    for copy in locals_:
+        copy.start()
+
+    causal = lax.broadcasted_iota(jnp.int32, (BLK, BLK), 0) <= lax.broadcasted_iota(
+        jnp.int32, (BLK, BLK), 1
+    )
+    for key_block in range(shards):
+        for query_block in range(shards):
+            hit = jnp.int32(0)
+            for m in range(slots.shape[1]):
+                same = (slots[query_block, m] == key_block) & (m < counts[query_block])
+                hit = hit | same.astype(jnp.int32)
+            if key_block > query_block:
+                hit = jnp.int32(0)
+            wide = jnp.full((BLK, BLK), hit, jnp.int32) > 0
+            if key_block == query_block:
+                wide = wide & causal
+            bias[key_block * BLK : (key_block + 1) * BLK,
+                 query_block * BLK : (query_block + 1) * BLK] = jnp.where(
+                     wide, 0.0, -1e30).astype(jnp.float32)
+    dlat[...] = jnp.zeros_like(dlat)
+    for copy in locals_:
+        copy.wait()
+    for d in peers:
+        lat_copy(d).wait()
+    for b in range(shards):
+        columns = slice(b * BLK, (b + 1) * BLK)
+        lat_t[:, columns] = lat_buf[b]
+        lat[columns, :] = lat_buf[b, :width, :].T
+        keys[columns, nope:query_width] = lat_buf[b, width:, :].T
+        keys_t[nope:, columns] = lat_buf[b, width:, :]
+
+    def one_head(h, unused):
+        @pl.when(h + AHEAD < heads)
+        def _():
+            send_head(h + AHEAD)
+
+        for d in peers:
+            q_copy(d, h).wait()
+            g_copy(d, h).wait()
+
+        def store_dq(block, value):
+            dq_buf[block, h] = value
+
+        latent_part, rope, k_grad, v_grad = head_math(
+            lambda b: q_buf[b, h], lambda b: g_buf[b, h], k_w[h], v_w[h], lat_t, lat, bias,
+            keys, keys_t, dk, dv, shards, store_dq
+        )
+        for d in peers:
+            dq_copy(d, h).start()
+        dq_own(h).start()
+        dlat[:width, :] += latent_part
+        dlat[width:, :] += rope
+        k_half[...] = k_grad
+        v_half[...] = v_grad
+        kx_out[h] = k_half[pl.ds((1 - rep) * k_rows, k_rows), :].astype(jnp.bfloat16)
+        vx_out[h] = v_half[pl.ds((1 - rep) * v_rows, v_rows), :].astype(jnp.bfloat16)
+        k_copy(h).start()
+        v_copy(h).start()
+        dk_out[h] = k_half[pl.ds(rep * k_rows, k_rows), :]
+        dv_out[h] = v_half[pl.ds(rep * v_rows, v_rows), :]
+        return unused
+
+    lax.fori_loop(0, heads, one_head, 0)
+
+    exchange = remote(dlat.at[pl.ds((1 - sub) * half_rows, half_rows), :], half_in,
+                      half_sem.at[0], half_sem.at[1], "sub", 1 - sub)
+    exchange.start()
+
+    def finish(h, unused):
+        k_copy(h).wait()
+        v_copy(h).wait()
+        dk_out[h] += kx_in[h].astype(jnp.float32)
+        dv_out[h] += vx_in[h].astype(jnp.float32)
+        return unused
+
+    exchange.wait()
+    half_in[...] += dlat[pl.ds(sub * half_rows, half_rows), :]
+    for b in range(shards):
+        piece_out[b] = half_in[:, b * BLK : (b + 1) * BLK].astype(jnp.bfloat16)
+
+    def piece_copy(d):
+        return remote(piece_out.at[peer(d)], piece_in.at[d - 1],
+                      piece_send.at[d - 1], piece_recv.at[d - 1], "seq", peer(d))
+
+    for d in peers:
+        piece_copy(d).start()
+    lax.fori_loop(0, heads, finish, 0)
+    gathered = half_in[:, pl.ds(pl.multiple_of(me * BLK, BLK), BLK)]
+    for d in peers:
+        piece_copy(d).wait()
+        gathered = gathered + piece_in[d - 1].astype(jnp.float32)
+    lat_out[...] = gathered
+
+    def drain(h, unused):
+        for d in peers:
+            dq_copy(d, h).wait()
+        dq_own(h).wait()
+        return unused
+
+    lax.fori_loop(0, heads, drain, 0)
+
+
+def local_small(queries, grad_out, latent_kv, key_up, value_up, key_blocks, block_counts):
+    shards = lax.axis_size("seq")
+    heads, _, nope, width = key_up.shape
+    value_width = value_up.shape[3]
+    q_t = jnp.transpose(queries[0], (1, 2, 0))
+    g_t = jnp.transpose(grad_out[0], (1, 0, 2))
+    lat_local = latent_kv[0].T
+    kv_width, tokens = lat_local.shape
+    total = shards * tokens
+    query_width = q_t.shape[1]
+    half = kv_width // 2
+    bf16, f32 = jnp.bfloat16, jnp.float32
+    hbm = pl.BlockSpec(memory_space=pl.ANY)
+    vmem = pl.BlockSpec(memory_space=pltpu.VMEM)
+    smem = pl.BlockSpec(memory_space=pltpu.SMEM)
+    sems = lambda *shape: pltpu.SemaphoreType.DMA(shape)
+    far = shards - 1
+    dq, dlat, dk, dv = pl.pallas_call(
+        functools.partial(attention_kernel, shards, heads),
+        in_specs=[smem, smem, hbm, hbm, hbm, hbm, hbm],
+        out_specs=[hbm, vmem, vmem, vmem],
+        out_shape=[
+            jax.ShapeDtypeStruct(q_t.shape, bf16),
+            jax.ShapeDtypeStruct((half, tokens), f32),
+            jax.ShapeDtypeStruct((heads, nope // 2, width), f32),
+            jax.ShapeDtypeStruct((heads, width // 2, value_width), f32),
+        ],
+        scratch_shapes=[
+            pltpu.VMEM((shards, heads, query_width, tokens), bf16),
+            pltpu.VMEM((shards, heads, tokens, value_width), bf16),
+            pltpu.VMEM((shards, kv_width, tokens), bf16),
+            pltpu.VMEM((heads, nope, width), bf16),
+            pltpu.VMEM((heads, width, value_width), bf16),
+            pltpu.VMEM((shards, heads, query_width, tokens), bf16),
+            pltpu.VMEM((kv_width, total), bf16),
+            pltpu.VMEM((total, width), bf16),
+            pltpu.VMEM((total, total), f32),
+            pltpu.VMEM((total, 2 * BLK), bf16),
+            pltpu.VMEM((query_width, total), bf16),
+            pltpu.VMEM((query_width, total), f32),
+            pltpu.VMEM((total, value_width), f32),
+            pltpu.VMEM((kv_width, total), f32),
+            pltpu.VMEM((nope, width), f32),
+            pltpu.VMEM((width, value_width), f32),
+            pltpu.VMEM((heads, nope // 2, width), bf16),
+            pltpu.VMEM((heads, nope // 2, width), bf16),
+            pltpu.VMEM((heads, width // 2, value_width), bf16),
+            pltpu.VMEM((heads, width // 2, value_width), bf16),
+            pltpu.VMEM((half, total), f32),
+            pltpu.VMEM((shards, half, tokens), bf16),
+            pltpu.VMEM((far, half, tokens), bf16),
+            sems(far, heads), sems(far, heads), sems(far, heads), sems(far, heads),
+            sems(far), sems(far),
+            sems(far, heads), sems(far, heads), sems(heads),
+            sems(2, heads), sems(2, heads), sems(2), sems(far), sems(far), sems(5),
+        ],
+        compiler_params=pltpu.CompilerParams(
+            collective_id=0, has_side_effects=True, vmem_limit_bytes=48 << 20
+        ),
+    )(key_blocks[0], block_counts[0], q_t, g_t, lat_local, key_up[:, 0], value_up[:, 0])
+    return (
+        jnp.transpose(dq, (2, 0, 1))[None],
+        dlat.T[None],
+        dk[:, None],
+        dv[:, None],
+    )
 
 
 def head_backward(
@@ -119,7 +432,7 @@
     return (grad_query, head_part, key_weight_grad, value_weight_grad)
 
 
-def local(queries, grad_out, latent_kv, key_up, value_up, key_blocks, block_counts):
+def local_general(queries, grad_out, latent_kv, key_up, value_up, key_blocks, block_counts):
     head_queries, head_grads = (
         lax.all_to_all(queries, "seq", split_axis=2, concat_axis=1, tiled=True),
         lax.all_to_all(grad_out, "seq", split_axis=2, concat_axis=1, tiled=True),
@@ -173,6 +486,19 @@
         P(("groups", "rep"), None, None),
         P(("groups", "rep"), None),
     )
+
+    def local(queries, grad_out, latent_kv, key_up, value_up, key_blocks, block_counts):
+        args = (queries, grad_out, latent_kv, key_up, value_up, key_blocks, block_counts)
+        shards = mesh.shape["seq"]
+        small = (
+            queries.shape[1] == BLK
+            and shards % 2 == 0
+            and shards * BLK <= 1024
+            and mesh.shape["rep"] == 2
+            and mesh.shape["sub"] == 2
+        )
+        return local_small(*args) if small else local_general(*args)
+
     return jax.shard_map(
         local,
         mesh=mesh,

time: 476 us -> 126 us (0.26)
  waiting for transfers between devices: 141 us -> 0 us
  Pallas kernels: 0 us -> 117 us
  matrix products: 89.5 us -> 0 us
  local copies, waits for them, and re-layouts: 92.8 us -> 8.72 us
  blocking collectives: 79.5 us -> 0 us
  other arithmetic: 39.7 us -> 0 us
  between operations: 15.5 us -> 0.7 us
  starting transfers between devices: 13.6 us -> 0 us
    all_to_all x3 -> x0, waiting for transfers between devices: 140 us -> none  [the longest x1 96.3 us: local(): lax.all_to_all(pieces, 'seq', split_axis=1, concat_axis=1, tiled=True)]
    pallas_call x0 -> x1, Pallas kernels: none -> 117 us  [local_small(): pl.pallas_call(functools.partial(attention_kernel, shards, heads), in_spe...]
    dot_general x96 -> x0, matrix products: 89.5 us -> none  [the longest x8 20.5 us: one_group(): jnp.einsum('gqk,gqd->gkd', probs_b, grad_tile, preferred_element_type=jnp...]
    all_gather x1 -> x0, blocking collectives: 47.7 us -> none  [local(): latent = lax.all_gather(latent_kv, 'seq', axis=1, tiled=True)[0]]
    all_to_all x1 -> x0, blocking collectives: 31.8 us -> none  [local(): lax.all_to_all(grad_out, 'seq', split_axis=2, concat_axis=1, tiled=True)]
    scatter-add x16 -> x0, other arithmetic: 25.2 us -> none  [the longest x8 14.2 us: one_group(): key_total.at[flat_slots]]
    dynamic_slice x18 -> x0, local copies, waits for them, and re-layouts: 20.1 us -> none  [the longest x16 16.6 us: local(): lax.scan(one_head, jnp.zeros((), jnp.float32), (query_stack, grad_stack,...]
    reshape x34 -> x0, local copies, waits for them, and re-layouts: 17.2 us -> none  [the longest x16 6.84 us: one_group(): grad_key.reshape(per_group * slot_count, block_rows, query_width)]
  transfers between devices with their start and end apart: 5 -> 0, of which waited for: 2 -> 0; matrix products, arithmetic and copies ran while one was open for 3% -> 0% of each run, Pallas kernels for 0% -> 0%
where the time goes in v2:
time: 126 us
  Pallas kernels  117 us (93%)
  local copies, waits for them, and re-layouts  8.72 us (7%)
    pallas_call x1, Pallas kernels, local_small(): pl.pallas_call(functools.partial(attention_kernel, shards, heads), in_spe...  117 us
    unnamed x14, local copies, waits for them, and re-layouts  8.72 us

profile of v2, /device:TPU:0, one launch (start us, length us, event | category | flops | bytes accessed | tf_op | source)
XLA Modules:
  0.0 126.3 jit_solution(10711232019645519434)
XLA Ops:
  0.6 0.0 copy-start.3
  0.6 0.0 copy-start.1
  0.7 0.0 copy-start
  0.7 0.9 copy.11
  1.6 1.6 %copy.16 = bf16[1,128,32,128]{3,1,2,0:T(8,128)(2,1)S(1)} copy(bf16[1,128,32,128]{3,2,1,0:T(8,128)(2,1)} %param.8) | data formatting | bytes 2097152 | tf_op args[1]
  3.2 0.0 copy-done.3
  3.2 0.0 copy-done.1
  3.2 0.0 copy-done
  3.2 0.0 copy-start.2
  3.3 0.9 copy-done.2
  4.2 116.8 %shard_map.102 = (bf16[32,192,128]{2,1,0:T(8,128)(2,1)}, f32[288,128]{1,0:T(8,128)S(1)}, f32[8,64,512]{2,1,0:T(8,128)S(1)}, f32[8,256,128]{2,1,0:T(8,128)S(1)}) custom-call(s32[4,3]{1,0:T(4,128)S(1)} %bitcast.34, s32[4]{0:T(128)S(1)} %bitcast.35, bf16[32,192,128]{2,1,0:T(8,128)(2,1)} %bitcast.37, bf16[32,128,128]{2,1,0:T(8,128)(2,1)S(1)} %bitcast.27, ...), custom_call_target="tpu_custom_call" | custom-call | tf_op jit(solution)/shard_map/pallas_call | solution.py:273
  121.0 2.7 %copy.21 = bf16[1,128,32,192]{1,3,2,0:T(8,128)(2,1)} copy(bf16[1,128,32,192]{1,3,2,0:T(8,128)(2,1)} %bitcast.36) | data formatting | bytes 3145728
  123.7 0.7 copy.22
  124.3 1.0 copy.23
  125.3 1.0 copy.24
Async XLA Ops:
  0.6 2.6 %copy-start.3 = (s32[1,4]{1,0:T(1,128)S(1)}, s32[1,4]{1,0:T(1,128)}, u32[]{:S(2)}) copy-start(s32[1,4]{1,0:T(1,128)} %param.13) | copy-start | bytes 52
  0.6 2.6 %copy-start.1 = (bf16[8,1,512,128]{3,2,1,0:T(8,128)(2,1)S(1)}, bf16[8,1,512,128]{3,2,1,0:T(8,128)(2,1)}, u32[]{:S(2)}) copy-start(bf16[8,1,512,128]{3,2,1,0:T(8,128)(2,1)} %param.11) | copy-start | bytes 3145732
  0.7 2.6 %copy-start = (bf16[8,1,128,512]{3,2,1,0:T(8,128)(2,1)S(1)}, bf16[8,1,128,512]{3,2,1,0:T(8,128)(2,1)}, u32[]{:S(2)}) copy-start(bf16[8,1,128,512]{3,2,1,0:T(8,128)(2,1)} %param.10) | copy-start | bytes 3145732
  3.2 0.9 copy-start.2

commit v3 on v2

--- a/solution.py
+++ b/solution.py
@@ -66,9 +66,10 @@
     slots, counts, q_in, g_in, lat_in, k_in, v_in,
     dq_out, lat_out, dk_out, dv_out,
     q_buf, g_buf, lat_buf, k_w, v_w, dq_buf, lat_t, lat, bias, keys, keys_t, dk, dv, dlat,
-    k_half, v_half, kx_out, kx_in, vx_out, vx_in, half_in, piece_out, piece_in,
+    k_half, v_half, kx_out, kx_in, vx_out, vx_in, half_in, piece_out, piece_in, cross_out, cross_in,
     q_send, q_recv, g_send, g_recv, lat_send, lat_recv, dq_send, dq_recv, dq_local,
     kx_sem, vx_sem, half_sem, piece_send, piece_recv, own_sem,
+    share_send, share_recv,
 ):
     me = lax.axis_index("seq")
     rep = lax.axis_index("rep")
@@ -81,6 +82,7 @@
     v_rows = vx_in.shape[1]
     half_rows = kv_width // 2
     peers = range(1, shards)
+    lat_rows = pl.ds(pl.multiple_of(sub * half_rows, 16), half_rows)
 
     def peer(d):
         return lax.rem(me + d, shards)
@@ -99,9 +101,21 @@
         return remote(g_in.at[peer(d) * heads + h], g_buf.at[me, h],
                       g_send.at[d - 1, h], g_recv.at[d - 1, h], "seq", peer(d))
 
-    def lat_copy(d):
-        return remote(lat_in, lat_buf.at[me], lat_send.at[d - 1], lat_recv.at[d - 1],
-                      "seq", peer(d))
+    near = me + 1 - 2 * lax.rem(me, 2)
+    cross = lax.rem(me + 2, 4)
+    diagonal = 3 - me
+
+    def lat_copy(slot, src, source, target):
+        return remote(src, lat_buf.at[source, lat_rows],
+                      lat_send.at[slot], lat_recv.at[slot], "seq", target)
+
+    lat_near = lat_copy(0, lat_in.at[lat_rows], me, near)
+    lat_cross = lat_copy(1, lat_in.at[lat_rows], me, cross)
+    lat_relay = lat_copy(2, lat_buf.at[cross, lat_rows], cross, near)
+
+    def share_copy(slot, source):
+        return remote(lat_buf.at[source, lat_rows], lat_buf.at[source, lat_rows],
+                      share_send.at[slot], share_recv.at[slot], "sub", 1 - sub)
 
     def dq_copy(d, h):
         return remote(dq_buf.at[peer(d), h], dq_out.at[me * heads + h],
@@ -129,8 +143,8 @@
                         device_id_type=pl.DeviceIdType.MESH)
     pl.semaphore_wait(barrier, shards + 1)
 
-    for d in peers:
-        lat_copy(d).start()
+    lat_cross.start()
+    lat_near.start()
 
     def send_head(h):
         for d in peers:
@@ -173,8 +187,16 @@
     dlat[...] = jnp.zeros_like(dlat)
     for copy in locals_:
         copy.wait()
-    for d in peers:
-        lat_copy(d).wait()
+    shares = [share_copy(0, near), share_copy(1, cross), share_copy(2, diagonal)]
+    lat_cross.wait()
+    lat_relay.start()
+    shares[1].start()
+    lat_near.wait()
+    shares[0].start()
+    lat_relay.wait()
+    shares[2].start()
+    for copy in shares:
+        copy.wait()
     for b in range(shards):
         columns = slice(b * BLK, (b + 1) * BLK)
         lat_t[:, columns] = lat_buf[b]
@@ -228,21 +250,22 @@
 
     exchange.wait()
     half_in[...] += dlat[pl.ds(sub * half_rows, half_rows), :]
-    for b in range(shards):
-        piece_out[b] = half_in[:, b * BLK : (b + 1) * BLK].astype(jnp.bfloat16)
-
-    def piece_copy(d):
-        return remote(piece_out.at[peer(d)], piece_in.at[d - 1],
-                      piece_send.at[d - 1], piece_recv.at[d - 1], "seq", peer(d))
-
-    for d in peers:
-        piece_copy(d).start()
+
+    def columns_of(block):
+        return half_in[:, pl.ds(pl.multiple_of(block * BLK, BLK), BLK)]
+
+    piece_out[0] = columns_of(near).astype(jnp.bfloat16)
+    piece_out[1] = columns_of(diagonal).astype(jnp.bfloat16)
+    beside = remote(piece_out, piece_in, piece_send.at[0], piece_recv.at[0], "seq", near)
+    beside.start()
+    beside.wait()
+    cross_out[...] = (columns_of(cross) + piece_in[1].astype(jnp.float32)).astype(jnp.bfloat16)
+    over = remote(cross_out, cross_in, piece_send.at[1], piece_recv.at[1], "seq", cross)
+    over.start()
     lax.fori_loop(0, heads, finish, 0)
-    gathered = half_in[:, pl.ds(pl.multiple_of(me * BLK, BLK), BLK)]
-    for d in peers:
-        piece_copy(d).wait()
-        gathered = gathered + piece_in[d - 1].astype(jnp.float32)
-    lat_out[...] = gathered
+    gathered = columns_of(me) + piece_in[0].astype(jnp.float32)
+    over.wait()
+    lat_out[...] = gathered + cross_in[...].astype(jnp.float32)
 
     def drain(h, unused):
         for d in peers:
@@ -302,12 +325,15 @@
             pltpu.VMEM((heads, width // 2, value_width), bf16),
             pltpu.VMEM((heads, width // 2, value_width), bf16),
             pltpu.VMEM((half, total), f32),
-            pltpu.VMEM((shards, half, tokens), bf16),
-            pltpu.VMEM((far, half, tokens), bf16),
+            pltpu.VMEM((2, half, tokens), bf16),
+            pltpu.VMEM((2, half, tokens), bf16),
+            pltpu.VMEM((half, tokens), bf16),
+            pltpu.VMEM((half, tokens), bf16),
             sems(far, heads), sems(far, heads), sems(far, heads), sems(far, heads),
             sems(far), sems(far),
             sems(far, heads), sems(far, heads), sems(heads),
-            sems(2, heads), sems(2, heads), sems(2), sems(far), sems(far), sems(5),
+            sems(2, heads), sems(2, heads), sems(2), sems(2), sems(2), sems(5),
+            sems(far), sems(far),
         ],
         compiler_params=pltpu.CompilerParams(
             collective_id=0, has_side_effects=True, vmem_limit_bytes=48 << 20
@@ -492,10 +518,10 @@
         shards = mesh.shape["seq"]
         small = (
             queries.shape[1] == BLK
-            and shards % 2 == 0
-            and shards * BLK <= 1024
+            and shards == 4
             and mesh.shape["rep"] == 2
             and mesh.shape["sub"] == 2
+            and latent_kv.shape[2] % 32 == 0
         )
         return local_small(*args) if small else local_general(*args)
 

time: 126 us -> 116 us (0.921)
  Pallas kernels: 117 us -> 106 us
    pallas_call x1, Pallas kernels: 117 us -> 106 us  [local_small(): pl.pallas_call(functools.partial(attention_kernel, shards, heads), in_spe...]
where the time goes in v3:
time: 116 us; the launch traced here: 115 us
  Pallas kernels  106 us (91%)
  local copies, waits for them, and re-layouts  8.72 us (8%)
    pallas_call x1, Pallas kernels, local_small(): pl.pallas_call(functools.partial(attention_kernel, shards, heads), in_spe...  106 us
    unnamed x14, local copies, waits for them, and re-layouts  8.72 us

profile of v3, /device:TPU:0, one launch (start us, length us, event | category | flops | bytes accessed | tf_op | source)
XLA Modules:
  0.0 115.4 jit_solution(5055983537614301611)
XLA Ops:
  0.6 0.0 copy-start.3
  0.6 0.0 copy-start.1
  0.7 0.0 copy-start
  0.7 0.9 copy.11
  1.6 1.6 %copy.16 = bf16[1,128,32,128]{3,1,2,0:T(8,128)(2,1)S(1)} copy(bf16[1,128,32,128]{3,2,1,0:T(8,128)(2,1)} %param.8) | data formatting | bytes 2097152 | tf_op args[1]
  3.2 0.0 copy-done.3
  3.2 0.0 copy-done.1
  3.2 0.0 copy-done
  3.2 0.0 copy-start.2
  3.3 0.9 copy-done.2
  4.2 106.0 %shard_map.102 = (bf16[32,192,128]{2,1,0:T(8,128)(2,1)}, f32[288,128]{1,0:T(8,128)S(1)}, f32[8,64,512]{2,1,0:T(8,128)S(1)}, f32[8,256,128]{2,1,0:T(8,128)S(1)}) custom-call(s32[4,3]{1,0:T(4,128)S(1)} %bitcast.34, s32[4]{0:T(128)S(1)} %bitcast.35, bf16[32,192,128]{2,1,0:T(8,128)(2,1)} %bitcast.37, bf16[32,128,128]{2,1,0:T(8,128)(2,1)S(1)} %bitcast.27, ...), custom_call_target="tpu_custom_call" | custom-call | tf_op jit(solution)/shard_map/pallas_call | solution.py:296
  110.2 2.7 %copy.21 = bf16[1,128,32,192]{1,3,2,0:T(8,128)(2,1)} copy(bf16[1,128,32,192]{1,3,2,0:T(8,128)(2,1)} %bitcast.36) | data formatting | bytes 3145728
  112.8 0.7 copy.22
  113.5 1.0 copy.23
  114.4 1.0 copy.24
Async XLA Ops:
  0.6 2.6 %copy-start.3 = (s32[1,4]{1,0:T(1,128)S(1)}, s32[1,4]{1,0:T(1,128)}, u32[]{:S(2)}) copy-start(s32[1,4]{1,0:T(1,128)} %param.13) | copy-start | bytes 52
  0.6 2.6 %copy-start.1 = (bf16[8,1,512,128]{3,2,1,0:T(8,128)(2,1)S(1)}, bf16[8,1,512,128]{3,2,1,0:T(8,128)(2,1)}, u32[]{:S(2)}) copy-start(bf16[8,1,512,128]{3,2,1,0:T(8,128)(2,1)} %param.11) | copy-start | bytes 3145732
  0.7 2.6 %copy-start = (bf16[8,1,128,512]{3,2,1,0:T(8,128)(2,1)S(1)}, bf16[8,1,128,512]{3,2,1,0:T(8,128)(2,1)}, u32[]{:S(2)}) copy-start(bf16[8,1,128,512]{3,2,1,0:T(8,128)(2,1)} %param.10) | copy-start | bytes 3145732
  3.2 0.9 copy-start.2

commit v4 on v3

--- a/solution.py
+++ b/solution.py
@@ -58,7 +58,7 @@
     return latent_part, rope, k_grad, v_grad
 
 
-AHEAD = 4
+AHEAD = 8
 
 
 def attention_kernel(
@@ -85,7 +85,7 @@
     lat_rows = pl.ds(pl.multiple_of(sub * half_rows, 16), half_rows)
 
     def peer(d):
-        return lax.rem(me + d, shards)
+        return (lax.rem(me + 2, 4), 3 - me, me + 1 - 2 * lax.rem(me, 2))[d - 1]
 
     def remote(src, dst, send, recv, axis, index):
         return pltpu.make_async_remote_copy(

time: 116 us -> 115 us (level)
  no operation moved by 1% of the time
where the time goes in v4:
time: 115 us; the launch traced here: 114 us
  Pallas kernels  105 us (91%)
  local copies, waits for them, and re-layouts  8.72 us (8%)
    pallas_call x1, Pallas kernels, local_small(): pl.pallas_call(functools.partial(attention_kernel, shards, heads), in_spe...  105 us
    unnamed x14, local copies, waits for them, and re-layouts  8.72 us

profile of v4, /device:TPU:0, one launch (start us, length us, event | category | flops | bytes accessed | tf_op | source)
XLA Modules:
  0.0 114.3 jit_solution(17015656066159074985)
XLA Ops:
  0.6 0.0 copy-start.3
  0.6 0.0 copy-start.1
  0.7 0.0 copy-start
  0.7 0.9 copy.11
  1.6 1.6 %copy.16 = bf16[1,128,32,128]{3,1,2,0:T(8,128)(2,1)S(1)} copy(bf16[1,128,32,128]{3,2,1,0:T(8,128)(2,1)} %param.8) | data formatting | bytes 2097152 | tf_op args[1]
  3.2 0.0 copy-done.3
  3.2 0.0 copy-done.1
  3.2 0.0 copy-done
  3.2 0.0 copy-start.2
  3.3 0.9 copy-done.2
  4.2 104.9 %shard_map.102 = (bf16[32,192,128]{2,1,0:T(8,128)(2,1)}, f32[288,128]{1,0:T(8,128)S(1)}, f32[8,64,512]{2,1,0:T(8,128)S(1)}, f32[8,256,128]{2,1,0:T(8,128)S(1)}) custom-call(s32[4,3]{1,0:T(4,128)S(1)} %bitcast.34, s32[4]{0:T(128)S(1)} %bitcast.35, bf16[32,192,128]{2,1,0:T(8,128)(2,1)} %bitcast.37, bf16[32,128,128]{2,1,0:T(8,128)(2,1)S(1)} %bitcast.27, ...), custom_call_target="tpu_custom_call" | custom-call | tf_op jit(solution)/shard_map/pallas_call | solution.py:296
  109.0 2.7 %copy.21 = bf16[1,128,32,192]{1,3,2,0:T(8,128)(2,1)} copy(bf16[1,128,32,192]{1,3,2,0:T(8,128)(2,1)} %bitcast.36) | data formatting | bytes 3145728
  111.7 0.7 copy.22
  112.4 1.0 copy.23
  113.3 1.0 copy.24
Async XLA Ops:
  0.6 2.6 %copy-start.3 = (s32[1,4]{1,0:T(1,128)S(1)}, s32[1,4]{1,0:T(1,128)}, u32[]{:S(2)}) copy-start(s32[1,4]{1,0:T(1,128)} %param.13) | copy-start | bytes 52
  0.6 2.6 %copy-start.1 = (bf16[8,1,512,128]{3,2,1,0:T(8,128)(2,1)S(1)}, bf16[8,1,512,128]{3,2,1,0:T(8,128)(2,1)}, u32[]{:S(2)}) copy-start(bf16[8,1,512,128]{3,2,1,0:T(8,128)(2,1)} %param.11) | copy-start | bytes 3145732
  0.7 2.6 %copy-start = (bf16[8,1,128,512]{3,2,1,0:T(8,128)(2,1)S(1)}, bf16[8,1,128,512]{3,2,1,0:T(8,128)(2,1)}, u32[]{:S(2)}) copy-start(bf16[8,1,128,512]{3,2,1,0:T(8,128)(2,1)} %param.10) | copy-start | bytes 3145732
  3.2 0.9 copy-start.2
